TPU v7x, 512 devices: a whole 4x8x8 slice. The times are simulated.
512 devices in a mesh: slab: 128 (over z, y, core), col: 4 (over x).
Axes of the slice: x: 4, y: 8, z: 8, core: 2. Of those that a mesh axis runs over, the one named last changes fastest.
Arguments:
- shot_boxes: int32 [4, 131072], P(None, ('slab', 'col')), may hold values from 0 to 8192, as said below
- shot_counts: int32 [128, 4], P('slab', 'col'), may hold values from 128 to 256, as said below
- shot_doses: float32 [131072], P(('slab', 'col')), may hold values from 0.2 to 1
- transfer: float32 [4096, 4096], P(('slab', 'col')), may hold values from 0.2 to 1
Outputs:
- dosage: float32 [131072], P(('slab', 'col'))
- exposure: float32 [8192, 8192], P('slab', 'col')
Inputs may be any that keep to these rules, and one draw needn't show every extreme that they name: `shot_boxes`: rows 0 to 3 hold a shot's first row, end row, first column and end column (ends exclusive); every shot covers one pixel or more. Slots are owned in blocks of 256 along slab+col; a shot's first row lies in its owner's 64 rows, its end row at most 64 rows further and never past the grid; its columns lie in its owner's 2048 columns, 64 at most. `shot_counts`: the first that many slots of each device are live, a multiple of 32; some device has all 256 live in every draw.
All inputs are finite; a program needn't handle non-finite values.
Results may differ from a plain program's by a relative error of at most 0.0023.
Values may be sent and summed in bfloat16 or wider, within the bound.
A program may use at most 128 MiB of HBM per device.

v0:
```python
import functools

import jax
import jax.numpy as jnp
import numpy as np
from jax import lax
from jax.experimental import pallas as pl
from jax.experimental.pallas import tpu as pltpu
from jax.sharding import PartitionSpec as P

HALO = 64
ITERS = 2
SLOTS = 256
ROWS = 64
COLS = 2048
LONG = 4096
NZ = 8
NYC = 16
N_SLAB = NZ * NYC
N_COL = 4
RELAX = 0.5
TARGET_LEVEL = 1.0
F32 = jnp.float32
BF16 = jnp.bfloat16
MESH = pl.DeviceIdType.MESH


def halves(values):
    high = np.asarray(values, np.float32).astype(jnp.bfloat16)
    low = (np.asarray(values, np.float64) - high.astype(np.float64)).astype(jnp.bfloat16)
    return high, low


def blur_taps():
    pos = np.arange(-HALO, HALO + 1).astype(np.float32)
    spread = np.float32(HALO / 3.0)
    raw = np.exp(np.float32(-0.5) * pos * pos / (spread * spread)).astype(np.float32)
    return (raw / raw.sum(dtype=np.float32)).astype(jnp.bfloat16)


@functools.lru_cache(None)
def tables():
    turn = 2.0 * np.pi
    yc, z, mm = np.meshgrid(np.arange(NYC), np.arange(NZ), np.arange(4), indexing="ij")
    freq = (4 * (NYC * z + yc) + mm).reshape(-1)
    angle = turn / 512 * ((freq[:, None] * np.arange(512)[None, :]) % 512)
    column = np.concatenate([np.cos(angle), np.sin(angle)], axis=1)
    slab_angle = turn / 128 * ((np.arange(128)[:, None] * np.arange(128)[None, :]) % 128)
    slab = np.concatenate([np.cos(slab_angle), np.sin(slab_angle)], axis=0)
    small = turn / 32 * ((np.arange(32)[:, None] * np.arange(32)[None, :]) % 32)
    cos, sin = np.cos(small), np.sin(small)
    forward = np.kron(np.eye(2), np.block([[cos, -sin], [sin, cos]]))
    backward = np.kron(np.eye(2), np.block([[cos, sin], [-sin, cos]]))
    lane = np.arange(128)
    twist = turn / LONG * (np.arange(128)[:, None] * (lane % 32)[None, :])
    sign = np.where(lane % 64 < 32, 1.0, -1.0)
    twists = np.stack([np.cos(twist), np.sin(twist) * sign]).astype(np.float32)
    classes = np.zeros((N_COL, 4, LONG), np.float32)
    for col in range(N_COL):
        for place, k in enumerate((col, 8 - col if col else 4)):
            theta = turn / LONG * ((np.arange(LONG) * k) % LONG)
            classes[col, 2 * place] = np.cos(theta)
            classes[col, 2 * place + 1] = np.sin(theta)
    taps = blur_taps()
    rows_band = np.zeros((ROWS, ROWS + 2 * HALO), jnp.bfloat16)
    for r in range(ROWS):
        rows_band[r, r : r + 2 * HALO + 1] = taps
    cols_band = np.zeros((384, 128), jnp.bfloat16)
    for c in range(128):
        cols_band[c + 64 : c + 64 + 2 * HALO + 1, c] = taps
    row_twice = (np.arange(ROWS)[:, None] // 2 == np.arange(32)[None, :]).astype(jnp.bfloat16)
    col_twice = (np.arange(128)[:, None] == np.arange(256)[None, :] // 2).astype(jnp.bfloat16)
    place = np.arange(512)
    regroup = np.zeros((512, 512), jnp.bfloat16)
    regroup[place, (place % 16) * 32 + place // 16] = 1
    return dict(
        column=np.stack(halves(column)),
        slab=np.stack(halves(slab)),
        small=np.stack(halves(forward) + halves(backward)),
        twists=twists,
        classes=classes,
        rows_band=rows_band,
        cols_band=cols_band,
        row_twice=row_twice,
        col_twice=col_twice,
        regroup=regroup,
        regroup_back=np.ascontiguousarray(regroup.T),
    )


NAMES = (
    "column",
    "slab",
    "small",
    "twists",
    "classes",
    "rows_band",
    "cols_band",
    "row_twice",
    "col_twice",
    "regroup",
    "regroup_back",
)


def mm(a, b, dims=((1,), (0,))):
    return lax.dot_general(a, b, (dims, ((), ())), preferred_element_type=F32)


def split(x):
    high = x.astype(BF16)
    return high, (x - high.astype(F32)).astype(BF16)


def swap_parts(x):
    lane = lax.broadcasted_iota(jnp.int32, x.shape, x.ndim - 1)
    return jnp.where(
        lane % 64 < 32,
        pltpu.roll(x, 96, x.ndim - 1),
        pltpu.roll(x, 32, x.ndim - 1),
    )


def kernel(
    pack_ref,
    transfer_ref,
    column_ref,
    slab_ref,
    small_ref,
    twists_ref,
    classes_ref,
    rows_band_ref,
    cols_band_ref,
    row_twice_ref,
    col_twice_ref,
    regroup_ref,
    regroup_back_ref,
    dosage_ref,
    exposure_ref,
    shots,
    doses,
    dose_out,
    spill,
    spill_out,
    t_rows,
    filt,
    cover,
    cover_side,
    cover_pool,
    weights,
    weights_side,
    extended,
    across,
    short,
    exposure_bf,
    coarse,
    uv,
    send1,
    recv1,
    send2,
    recv2,
    back2_out,
    back2,
    back1_out,
    back1,
    field_out,
    field,
    shot_send,
    shot_recv,
    dose_send,
    dose_recv,
    t_send,
    t_recv,
    y_send,
    y_recv,
    z_send,
    z_recv,
    x_send,
    x_recv,
    spill_sems,
):
    s = lax.axis_index("slab")
    c = lax.axis_index("col")
    z = s // NYC
    yc = s % NYC

    def near(offset, col):
        return (lax.rem(s + offset + N_SLAB, N_SLAB), col)

    def remote(src, dst, send_sem, recv_sem, device):
        return pltpu.make_async_remote_copy(
            src_ref=src,
            dst_ref=dst,
            send_sem=send_sem,
            recv_sem=recv_sem,
            device_id=device,
            device_id_type=MESH,
        )

    barrier = pltpu.get_barrier_semaphore()
    for offset in range(-2, 3):
        for step in range(N_COL):
            if offset or step:
                pl.semaphore_signal(
                    barrier,
                    inc=1,
                    device_id=near(offset, lax.rem(c + step, N_COL)),
                    device_id_type=MESH,
                )

    def greet_y(step, carry):
        there = z * NYC + lax.rem(yc + step, NYC)
        pl.semaphore_signal(barrier, inc=1, device_id=(there, c), device_id_type=MESH)
        return carry

    def greet_z(step, carry):
        there = lax.rem(z + step, NZ) * NYC + yc
        pl.semaphore_signal(barrier, inc=1, device_id=(there, c), device_id_type=MESH)
        return carry

    lax.fori_loop(1, NYC, greet_y, 0)
    lax.fori_loop(1, NZ, greet_z, 0)
    pl.semaphore_wait(barrier, 19 + NYC - 1 + NZ - 1)

    def to_near(source, target, sends, recvs):
        out = []
        for d in range(4):
            for step in range(N_COL):
                if d != 2 or step:
                    out.append(
                        remote(
                            source,
                            target.at[4 * d + c],
                            sends.at[4 * d + step],
                            recvs.at[4 * d + c],
                            near(2 - d, lax.rem(c + step, N_COL)),
                        )
                    )
        return out

    def from_near(source, target, sends, recvs):
        for d in range(4):
            for step in range(N_COL):
                if d != 2 or step:
                    slot = 4 * d + lax.rem(c + step, N_COL)
                    remote(
                        source, target.at[slot], sends.at[0], recvs.at[slot], (s, c)
                    ).wait_recv()

    shot_copies = to_near(pack_ref, shots, shot_send, shot_recv)
    for copy in shot_copies:
        copy.start()

    def class_row(col, place):
        return col if place == 0 else 4 + lax.rem(4 - col, 4)

    t_copies = []
    for step in range(1, N_COL):
        col = lax.rem(c + step, N_COL)
        for place in range(2):
            t_copies.append(
                remote(
                    transfer_ref.at[class_row(col, place)],
                    t_rows.at[2 * c + place],
                    t_send.at[2 * step + place],
                    t_recv.at[2 * c + place],
                    (s, col),
                )
            )
    for copy in t_copies:
        copy.start()
    for place in range(2):
        t_rows[2 * c + place] = transfer_ref[class_row(c, place)]
    shots[8 + c] = pack_ref[...]
    from_near(pack_ref, shots, shot_send, shot_recv)

    def pool_cover(col, carry):
        for d in (1, 2):
            box = jnp.transpose(shots[4 * d + col])
            start = jnp.broadcast_to(box[:, 2:3], (SLOTS, 128))
            end = jnp.broadcast_to(box[:, 3:4], (SLOTS, 128))

            def one(block, inner):
                lane = lax.broadcasted_iota(jnp.int32, (SLOTS, 128), 1) + block * 128
                left = (2 * lane + col * COLS).astype(F32)
                part = jnp.minimum(end, left + 2.0) - jnp.maximum(start, left)
                at = pl.multiple_of(block * 128, 128)
                cover_pool[col, (d - 1) * SLOTS : d * SLOTS, pl.ds(at, 128)] = jnp.maximum(
                    part, 0.0
                ).astype(BF16)
                return inner

            lax.fori_loop(0, 8, one, 0)
        return carry

    lax.fori_loop(0, N_COL, pool_cover, 0)

    def full_covers():
        for d in range(4):
            box = jnp.transpose(shots[4 * d + c])
            start = jnp.broadcast_to(box[:, 2:3], (SLOTS, 128))
            end = jnp.broadcast_to(box[:, 3:4], (SLOTS, 128))
            rows = slice(d * SLOTS, (d + 1) * SLOTS)

            def one(block, inner):
                lane = lax.broadcasted_iota(jnp.int32, (SLOTS, 128), 1) + block * 128
                pos = (lane + c * COLS).astype(F32)
                inside = (pos >= start) & (pos < end)
                at = pl.multiple_of(block * 128, 128)
                cover[rows, pl.ds(at, 128)] = jnp.where(inside, 1.0, 0.0).astype(BF16)
                return inner

            lax.fori_loop(0, COLS // 128, one, 0)
            for side in range(2):
                other = lax.rem(c + (1 if side else 3), N_COL)
                box = jnp.transpose(shots[4 * d + other])
                lane = lax.broadcasted_iota(jnp.int32, (SLOTS, 128), 1)
                pos = (lane + c * COLS + (COLS if side else -128)).astype(F32)
                inside = (pos >= box[:, 2:3]) & (pos < box[:, 3:4])
                cover_side[side, rows, :] = jnp.where(inside, 1.0, 0.0).astype(BF16)

    def make_filter():
        for step in range(1, N_COL):
            for place in range(2):
                slot = 2 * lax.rem(c + step, N_COL) + place
                remote(
                    transfer_ref.at[0], t_rows.at[slot], t_send.at[0], t_recv.at[slot], (s, c)
                ).wait_recv()
        for line in range(4):
            first, second = t_rows[2 * line], t_rows[2 * line + 1]
            stack = jnp.concatenate([first, first, second, second], axis=0)
            filt[line] = jnp.transpose(stack) * (1.0 / (LONG * LONG))

    box_own = pack_ref[...]
    dose = box_own[4:5]
    live = dose > 0.0
    area = (box_own[1:2] - box_own[0:1]) * (box_own[3:4] - box_own[2:3])
    lane_in = lax.broadcasted_iota(jnp.int32, (128, 512), 1)

    for iteration in range(ITERS):

        def dose_of(slot):
            if iteration == 0:
                value = shots[slot, 4:5, :]
            else:
                value = doses[slot]
            return value.astype(BF16).astype(F32)

        for col in range(N_COL):
            parts = []
            for d in (1, 2):
                slot = 4 * d + col
                top = 2 * lax.broadcasted_iota(jnp.int32, (32, SLOTS), 0) + s * ROWS
                top = top.astype(F32)
                part = jnp.minimum(shots[slot, 1:2, :], top + 2.0) - jnp.maximum(
                    shots[slot, 0:1, :], top
                )
                parts.append(jnp.maximum(part, 0.0) * (dose_of(slot) * 0.25))
            row_part = jnp.concatenate(parts, axis=1).astype(BF16)
            coarse[:, col * 1024 : (col + 1) * 1024] = mm(row_part, cover_pool[col])

        class_table = classes_ref[c]
        for place in range(2):
            real = jnp.zeros((32, 512), F32)
            imag = jnp.zeros((32, 512), F32)
            for q in range(8):
                block = slice(q * 512, (q + 1) * 512)
                x = coarse[:, block]
                real = real + x * class_table[2 * place : 2 * place + 1, block]
                imag = imag - x * class_table[2 * place + 1 : 2 * place + 2, block]
            at = place * 64
            for start, value in ((0, real), (32, imag)):
                high, low = split(value)
                uv[at + start : at + start + 32, 0:512] = high
                uv[128 + at + start : 128 + at + start + 32, 0:512] = low
            for start, value in ((0, imag), (32, -real)):
                high, low = split(value)
                uv[at + start : at + start + 32, 512:1024] = high
                uv[128 + at + start : 128 + at + start + 32, 512:1024] = low
        both = mm(column_ref[0], uv[...], ((1,), (1,)))
        spectrum = (
            both[:, :128] + both[:, 128:] + mm(column_ref[1], uv[0:128, :], ((1,), (1,)))
        )
        send1[iteration] = spectrum.astype(BF16).reshape(NYC, 32, 128)

        def y_copy(step, source, target):
            there = lax.rem(yc + step, NYC)
            return remote(
                source.at[iteration, there],
                target.at[iteration, yc],
                y_send.at[step],
                y_recv.at[(1 if target is back1 else 0) * ITERS + iteration, yc],
                (z * NYC + there, c),
            )

        def z_copy(step, source, target):
            there = lax.rem(z + step, NZ)
            return remote(
                source.at[iteration, there],
                target.at[iteration, z],
                z_send.at[step],
                z_recv.at[(1 if target is back2 else 0) * ITERS + iteration, z],
                (there * NYC + yc, c),
            )

        def begin(count, make, source, target, own):
            def go(step, carry):
                make(step, source, target).start()
                return carry

            lax.fori_loop(1, count, go, 0)
            target[iteration, own] = source[iteration, own]

        def finish(count, make, source, target, own, recvs, which):
            def go(step, carry):
                make(step, source, target).wait_send()
                slot = lax.rem(own + step, count)
                remote(
                    source.at[iteration, slot],
                    target.at[iteration, slot],
                    recvs.at[0, 0],
                    recvs.at[which * ITERS + iteration, slot],
                    (s, c),
                ).wait_recv()
                return carry

            lax.fori_loop(1, count, go, 0)

        begin(NYC, y_copy, send1, recv1, yc)

        if iteration == 0:
            full_covers()
        row_pos = (
            lax.broadcasted_iota(jnp.int32, (3 * ROWS, SLOTS), 0) + (s * ROWS - ROWS)
        ).astype(F32)
        for d in range(4):
            lanes = slice(d * SLOTS, (d + 1) * SLOTS)
            for place, step in enumerate((0, 3, 1)):
                slot = 4 * d + lax.rem(c + step, N_COL)
                inside = (row_pos >= shots[slot, 0:1, :]) & (row_pos < shots[slot, 1:2, :])
                value = jnp.where(inside, dose_of(slot), 0.0).astype(BF16)
                if place:
                    weights_side[place - 1, :, lanes] = value
                else:
                    weights[:, lanes] = value
        for side in range(2):
            at = side * (COLS + 128)
            block = mm(weights_side[side], cover_side[side]).astype(BF16)
            extended[:, at : at + 128] = block
            across[:, at : at + 128] = mm(rows_band_ref[...], block).astype(BF16)

        def raster(block, carry):
            at = pl.multiple_of(block * 256, 256)
            tile = mm(weights[...], cover[:, pl.ds(at, 256)]).astype(BF16)
            across[:, pl.ds(at + 128, 256)] = mm(rows_band_ref[...], tile).astype(BF16)
            return carry

        lax.fori_loop(0, COLS // 256, raster, 0)

        finish(NYC, y_copy, send1, recv1, yc, y_recv, 0)
        moved = mm(regroup_ref[...], recv1[iteration].reshape(512, 128)).astype(BF16)
        send2[iteration] = moved.reshape(NZ, 64, 128)
        begin(NZ, z_copy, send2, recv2, z)

        def blur(block, carry):
            at = pl.multiple_of(block * 128, 128)
            short[:, pl.ds(at, 128)] = mm(across[:, pl.ds(at, 384)], cols_band_ref[...])
            return carry

        lax.fori_loop(0, COLS // 128, blur, 0)
        if iteration == 0:
            make_filter()

        finish(NZ, z_copy, send2, recv2, z, z_recv, 0)

        lines = jnp.concatenate(
            [
                recv2[iteration, :, line * 16 : (line + 1) * 16, :].reshape(128, 128)
                for line in range(4)
            ],
            axis=1,
        )
        both = mm(slab_ref[0], lines) + mm(slab_ref[1], lines)
        cos_twist, sin_twist = twists_ref[0], twists_ref[1]
        sign = jnp.where(lax.broadcasted_iota(jnp.int32, (128, 128), 1) % 64 < 32, 1.0, -1.0)
        turned = []
        for line in range(4):
            lanes = slice(line * 128, (line + 1) * 128)
            value = both[:128, lanes] + sign * swap_parts(both[128:, lanes])
            turned.append(value * cos_twist + swap_parts(value) * sin_twist)
        value = jnp.concatenate(turned, axis=0)
        high, low = split(value)
        value = mm(high, small_ref[0]) + mm(low, small_ref[0]) + mm(high, small_ref[1])
        value = value * filt[...].reshape(512, 128)
        high, low = split(value)
        value = mm(high, small_ref[2]) + mm(low, small_ref[2]) + mm(high, small_ref[3])
        turned = []
        for line in range(4):
            part = value[line * 128 : (line + 1) * 128]
            turned.append(part * cos_twist - swap_parts(part) * sin_twist)
        value = jnp.concatenate(turned, axis=1)
        high, low = split(value)
        both = mm(slab_ref[0], high) + mm(slab_ref[0], low) + mm(slab_ref[1], high)
        for line in range(4):
            lanes = slice(line * 128, (line + 1) * 128)
            part = both[:128, lanes] - sign * swap_parts(both[128:, lanes])
            back2_out[iteration, :, line * 16 : (line + 1) * 16, :] = part.astype(BF16).reshape(
                NZ, 16, 128
            )
        begin(NZ, z_copy, back2_out, back2, z)
        finish(NZ, z_copy, back2_out, back2, z, z_recv, 1)
        moved = mm(regroup_back_ref[...], back2[iteration].reshape(512, 128)).astype(BF16)
        back1_out[iteration] = moved.reshape(NYC, 32, 128)
        begin(NYC, y_copy, back1_out, back1, yc)
        finish(NYC, y_copy, back1_out, back1, yc, y_recv, 1)

        held = back1[iteration].reshape(512, 128)
        both = mm(held, column_ref[0], ((0,), (0,))) + mm(held, column_ref[1], ((0,), (0,)))
        points = []
        for place in range(2):
            re = slice(place * 64, place * 64 + 32)
            im = slice(place * 64 + 32, place * 64 + 64)
            points.append(
                (both[re, :512] - both[im, 512:], both[re, 512:] + both[im, :512])
            )
        for q in range(8):
            block = slice(q * 512, (q + 1) * 512)
            total = jnp.zeros((32, 512), F32)
            for place in range(2):
                total = total + (
                    points[place][0] * class_table[2 * place : 2 * place + 1, block]
                    - points[place][1] * class_table[2 * place + 1 : 2 * place + 2, block]
                )
            at = (q % 2) * 512
            field_out[iteration, q // 2, :, at : at + 512] = total.astype(BF16)
        x_copies = []
        for step in range(1, N_COL):
            col = lax.rem(c + step, N_COL)
            x_copies.append(
                remote(
                    field_out.at[iteration, col],
                    field.at[iteration, c],
                    x_send.at[step],
                    x_recv.at[iteration, c],
                    (s, col),
                )
            )
        for copy in x_copies:
            copy.start()
        back = field_out[iteration, c].astype(F32)
        for step in range(1, N_COL):
            slot = lax.rem(c + step, N_COL)
            remote(
                field_out.at[iteration, slot],
                field.at[iteration, slot],
                x_send.at[0],
                x_recv.at[iteration, slot],
                (s, c),
            ).wait_recv()
            back = back + field[iteration, slot].astype(F32)
        for copy in x_copies:
            copy.wait_send()

        high, low = split(back)
        high = mm(row_twice_ref[...], high).astype(BF16)
        low = mm(row_twice_ref[...], low).astype(BF16)
        for block in range(8):
            lanes = slice(block * 128, (block + 1) * 128)
            wide = slice(block * 256, (block + 1) * 256)
            value = (
                short[:, wide]
                + mm(high[:, lanes], col_twice_ref[...])
                + mm(low[:, lanes], col_twice_ref[...])
            )
            if iteration == ITERS - 1:
                exposure_ref[:, wide] = value
            exposure_bf[:, wide] = value.astype(BF16)

        sums = mm(exposure_bf[...], cover[SLOTS : 3 * SLOTS, :], ((1,), (1,)))
        row_pos = (lax.broadcasted_iota(jnp.int32, (ROWS, SLOTS), 0) + s * ROWS).astype(F32)
        found = []
        for d in (1, 2):
            slot = 4 * d + c
            inside = (row_pos >= shots[slot, 0:1, :]) & (row_pos < shots[slot, 1:2, :])
            part = jnp.where(inside, sums[:, (d - 1) * SLOTS : d * SLOTS], 0.0)
            found.append(jnp.sum(part, axis=0, keepdims=True))
        spill_out[iteration] = found[0]
        copy = remote(
            spill_out.at[iteration],
            spill.at[iteration],
            spill_sems.at[0, iteration],
            spill_sems.at[1, iteration],
            near(-1, c),
        )
        copy.start()
        copy.wait()
        average = (found[1] + spill[iteration]) / area
        dose = jnp.where(live, dose * jnp.exp(RELAX * (TARGET_LEVEL - average)), 0.0)
        if iteration == 0:
            dose_out[...] = dose
            dose_copies = to_near(dose_out, doses, dose_send, dose_recv)
            for copy in dose_copies:
                copy.start()
            doses[8 + c] = dose
            from_near(dose_out, doses, dose_send, dose_recv)
            for copy in dose_copies + shot_copies + t_copies:
                copy.wait_send()
    dosage_ref[...] = dose


def per_device(shot_boxes, shot_counts, shot_doses, transfer):
    live = jnp.arange(SLOTS, dtype=jnp.int32) < shot_counts[0, 0]
    dosage = jnp.where(live, shot_doses, 0.0)
    pack = jnp.concatenate(
        [shot_boxes.astype(F32), jnp.broadcast_to(dosage[None], (4, SLOTS))], axis=0
    )
    t = tables()
    constants = [jnp.asarray(t[name]) for name in NAMES]
    vmem = pl.BlockSpec(memory_space=pltpu.VMEM)
    dma = pltpu.SemaphoreType.DMA
    dosage, exposure = pl.pallas_call(
        kernel,
        out_shape=(
            jax.ShapeDtypeStruct((1, SLOTS), F32),
            jax.ShapeDtypeStruct((ROWS, COLS), F32),
        ),
        in_specs=[vmem] * (2 + len(constants)),
        out_specs=(vmem, vmem),
        scratch_shapes=[
            pltpu.VMEM((16, 8, SLOTS), F32),
            pltpu.VMEM((16, 1, SLOTS), F32),
            pltpu.VMEM((1, SLOTS), F32),
            pltpu.VMEM((ITERS, 1, SLOTS), F32),
            pltpu.VMEM((ITERS, 1, SLOTS), F32),
            pltpu.VMEM((8, 32, 128), F32),
            pltpu.VMEM((4, 128, 128), F32),
            pltpu.VMEM((4 * SLOTS, COLS), BF16),
            pltpu.VMEM((2, 4 * SLOTS, 128), BF16),
            pltpu.VMEM((N_COL, 2 * SLOTS, 1024), BF16),
            pltpu.VMEM((3 * ROWS, 4 * SLOTS), BF16),
            pltpu.VMEM((2, 3 * ROWS, 4 * SLOTS), BF16),
            pltpu.VMEM((3 * ROWS, COLS + 256), BF16),
            pltpu.VMEM((ROWS, COLS + 256), BF16),
            pltpu.VMEM((ROWS, COLS), F32),
            pltpu.VMEM((ROWS, COLS), BF16),
            pltpu.VMEM((32, LONG), F32),
            pltpu.VMEM((256, 1024), BF16),
            pltpu.VMEM((ITERS, NYC, 32, 128), BF16),
            pltpu.VMEM((ITERS, NYC, 32, 128), BF16),
            pltpu.VMEM((ITERS, NZ, 64, 128), BF16),
            pltpu.VMEM((ITERS, NZ, 64, 128), BF16),
            pltpu.VMEM((ITERS, NZ, 64, 128), BF16),
            pltpu.VMEM((ITERS, NZ, 64, 128), BF16),
            pltpu.VMEM((ITERS, NYC, 32, 128), BF16),
            pltpu.VMEM((ITERS, NYC, 32, 128), BF16),
            pltpu.VMEM((ITERS, N_COL, 32, 1024), BF16),
            pltpu.VMEM((ITERS, N_COL, 32, 1024), BF16),
            dma((16,)),
            dma((16,)),
            dma((16,)),
            dma((16,)),
            dma((8,)),
            dma((8,)),
            dma((NYC,)),
            dma((2 * ITERS, NYC)),
            dma((NZ,)),
            dma((2 * ITERS, NZ)),
            dma((N_COL,)),
            dma((ITERS, N_COL)),
            dma((2, ITERS)),
        ],
        compiler_params=pltpu.CompilerParams(
            collective_id=0, has_side_effects=True, vmem_limit_bytes=48 << 20
        ),
        name="dose_correction",
    )(pack, transfer.reshape(8, 32, 128), *constants)
    return dosage.reshape(SLOTS), exposure


def solution(mesh):
    placed = (
        P(None, ("slab", "col")),
        P("slab", "col"),
        P(("slab", "col")),
        P(("slab", "col"), None),
    )
    return jax.shard_map(
        per_device,
        mesh=mesh,
        in_specs=placed,
        out_specs=(P(("slab", "col")), P("slab", "col")),
        check_vma=False,
    )
```

profile of v0, /device:TPU:1, one launch (start us, length us, event | category | flops | bytes accessed | tf_op | source)
XLA Modules:
  0.0 123.9 jit_solution(8760665901192667061)
XLA Ops:
  1.3 0.7 compare_select_fusion
  2.0 0.7 convert_element_type.3
  2.7 0.9 copy.19
  3.6 0.0 copy-start
  3.6 1.6 %copy-done = bf16[2,512,1024]{2,1,0:T(8,128)(2,1)S(1)} copy-done((bf16[2,512,1024]{2,1,0:T(8,128)(2,1)S(1)}, bf16[2,512,1024]{2,1,0:T(8,128)(2,1)}, u32[]{:S(2)}) %copy-start) | copy-done | bytes 2097176
  5.2 0.0 copy-start.1
  5.2 1.0 copy-done.1
  6.2 1.0 copy-done.2
  7.3 0.0 copy-start.3
  7.3 0.9 copy-done.3
  8.2 0.0 copy-start.4
  8.2 0.9 copy-done.4
  9.1 0.0 copy-start.5
  9.1 0.9 copy-done.5
  10.0 0.0 copy-start.6
  10.0 0.9 copy-done.6
  10.9 0.0 copy-start.7
  10.9 0.9 copy-done.7
  11.8 0.8 copy-done.8
  12.7 0.8 copy-done.9
  13.4 0.7 copy-done.10
  14.2 108.4 %dose_correction.1 = (f32[1,256]{1,0:T(1,128)S(1)}, f32[64,2048]{1,0:T(8,128)S(1)}) custom-call(f32[8,256]{1,0:T(8,128)S(1)} %pad_maximum_fusion.pack_ref, f32[8,32,128]{2,1,0:T(8,128)S(1)} %bitcast.7, bf16[2,512,1024]{2,1,0:T(8,128)(2,1)S(1)} %copy-done, bf16[2,256,128]{2,1,0:T(8,128)(2,1)S(1)} %copy-done.6, bf16[4,128,128]{2,1,0:T(8,128)(2,1)S(1)} %copy-done.5, ...), custom_call_target="tpu_custom_call" | custom-call | tf_op jit(solution)/shard_map/dose_correction/pallas_call | solution.py:621
  122.5 0.6 copy.23
  123.1 0.8 copy.24
  (6 shorter events, 0.0 us)
Async XLA Ops:
  3.6 1.6 %copy-start = (bf16[2,512,1024]{2,1,0:T(8,128)(2,1)S(1)}, bf16[2,512,1024]{2,1,0:T(8,128)(2,1)}, u32[]{:S(2)}) copy-start(bf16[2,512,1024]{2,1,0:T(8,128)(2,1)} %constant.24.clone.column_ref) | copy-start | bytes 6291460
  5.2 1.0 copy-start.1
  6.2 1.0 copy-start.2
  7.3 0.9 copy-start.3
  8.2 0.9 copy-start.4
  9.1 0.9 copy-start.5
  10.0 0.9 copy-start.6
  10.9 0.9 copy-start.7
  11.8 0.8 copy-start.8
  12.7 0.8 copy-start.9
  13.4 0.7 copy-start.10
where the time goes:
time: 124 us
  Pallas kernels  108 us (87%)
  local copies, waits for them, and re-layouts  12.8 us (10%)
  other arithmetic  1.38 us (1%)
  between operations  1.31 us (1%)
    pallas_call x1, Pallas kernels, per_device(): pl.pallas_call(kernel, out_shape=(jax.ShapeDtypeStruct((1, SLOTS), F32),...  108 us
    unnamed x25, local copies, waits for them, and re-layouts  12.8 us

commit v1 on v0

v1 whole, which is shorter than its diff:
```python
import functools
import math

import jax
import jax.numpy as jnp
import numpy as np
from jax import lax
from jax.experimental import pallas as pl
from jax.experimental.pallas import tpu as pltpu
from jax.sharding import PartitionSpec as P

HALO = 64
ITERS = 2
SLOTS = 256
ROWS = 64
COLS = 2048
LONG = 4096
N_SLAB = 128
N_COL = 4
RELAX = 0.5
TARGET_LEVEL = 1.0
F32 = jnp.float32
BF16 = jnp.bfloat16
MESH = pl.DeviceIdType.MESH


def halves(values):
    high = np.asarray(values, np.float32).astype(jnp.bfloat16)
    low = (np.asarray(values, np.float64) - high.astype(np.float64)).astype(jnp.bfloat16)
    return high, low


def blur_taps():
    pos = np.arange(-HALO, HALO + 1).astype(np.float32)
    spread = np.float32(HALO / 3.0)
    raw = np.exp(np.float32(-0.5) * pos * pos / (spread * spread)).astype(np.float32)
    return (raw / raw.sum(dtype=np.float32)).astype(jnp.bfloat16)


@functools.lru_cache(None)
def tables():
    turn = 2.0 * np.pi
    angle = turn / 512 * ((np.arange(256)[:, None] * np.arange(512)[None, :]) % 512)
    column = np.concatenate([np.cos(angle), np.sin(angle)], axis=1)
    slab_angle = turn / 128 * ((np.arange(128)[:, None] * np.arange(128)[None, :]) % 128)
    pair = np.eye(2)
    slab = np.concatenate([np.kron(np.cos(slab_angle), pair), np.kron(np.sin(slab_angle), pair)])
    small = turn / 32 * ((np.arange(32)[:, None] * np.arange(32)[None, :]) % 32)
    cos, sin = np.cos(small), np.sin(small)
    forward = np.kron(pair, np.block([[cos, -sin], [sin, cos]]))
    backward = np.kron(pair, np.block([[cos, sin], [-sin, cos]]))
    lane = np.arange(128)
    scale = 2.0 ** ((lane % 32) / 32.0)
    twist = turn / LONG * np.repeat(np.arange(128), 2)[:, None] * (lane % 32)[None, :]
    sign = np.where(lane % 64 < 32, 1.0, -1.0)
    twists = np.stack(
        [
            np.cos(twist) / scale,
            np.sin(twist) * sign / scale,
            np.cos(twist) * scale,
            np.sin(twist) * sign * scale,
        ]
    ).astype(np.float32)
    classes = np.zeros((N_COL, 4, LONG), np.float32)
    for col in range(N_COL):
        for place, k in enumerate((col, col + 2048) if col else (0, 4)):
            theta = turn / LONG * ((np.arange(LONG) * k) % LONG)
            classes[col, 2 * place] = np.cos(theta)
            classes[col, 2 * place + 1] = np.sin(theta)
    taps = blur_taps()
    rows_band = np.zeros((ROWS, ROWS + 2 * HALO), jnp.bfloat16)
    for r in range(ROWS):
        rows_band[r, r : r + 2 * HALO + 1] = taps
    cols_band = np.zeros((384, 128), jnp.bfloat16)
    for c in range(128):
        cols_band[c + 64 : c + 64 + 2 * HALO + 1, c] = taps
    row_twice = (np.arange(ROWS)[:, None] // 2 == np.arange(32)[None, :]).astype(jnp.bfloat16)
    col_twice = (np.arange(128)[:, None] == np.arange(256)[None, :] // 2).astype(jnp.bfloat16)
    alternate = np.zeros((16, 512), jnp.bfloat16)
    alternate[0] = 1 - 2 * (np.arange(512) % 2)
    scales = np.stack([scale, np.zeros(128)] * 4).astype(np.float32)
    return dict(
        column=np.stack(halves(column)),
        slab=np.stack(halves(slab)),
        small=np.stack(halves(forward) + halves(backward)),
        twists=twists,
        classes=classes,
        rows_band=rows_band,
        cols_band=cols_band,
        row_twice=row_twice,
        col_twice=col_twice,
        alternate=alternate,
        scales=scales,
    )


NAMES = (
    "column",
    "slab",
    "small",
    "twists",
    "classes",
    "rows_band",
    "cols_band",
    "row_twice",
    "col_twice",
    "alternate",
    "scales",
)


def mm(a, b, dims=((1,), (0,))):
    return lax.dot_general(a, b, (dims, ((), ())), preferred_element_type=F32)


def split(x):
    high = x.astype(BF16)
    return high, (x - high.astype(F32)).astype(BF16)


def swap_parts(x):
    lane = lax.broadcasted_iota(jnp.int32, x.shape, x.ndim - 1)
    return jnp.where(
        lane % 64 < 32,
        pltpu.roll(x, 96, x.ndim - 1),
        pltpu.roll(x, 32, x.ndim - 1),
    )


def kernel(
    boxes_in,
    counts_in,
    doses_in,
    transfer_ref,
    *rest,
):
    constants_in = dict(zip(NAMES, rest[: len(NAMES)]))
    rest = rest[len(NAMES) :]
    dosage_ref, exposure_ref = rest[:2]
    held_in = dict(zip(NAMES, rest[2 : 2 + len(NAMES)]))
    (
        boxes,
        counts,
        doses_own,
        pack,
        shots,
        doses,
        sums_out,
        sums,
        spill,
        t_rows,
        filt,
        mix,
        cover,
        cover_side,
        cover_pool,
        weights,
        weights_side,
        across,
        short,
        exposure_bf,
        coarse,
        uv,
        send1,
        recv1,
        send2,
        recv2,
        field_out,
        field,
        const_sems,
        in_sems,
        shot_send,
        shot_recv,
        sums_send,
        sums_recv,
        t_send,
        t_recv,
        slab_send,
        slab_recv,
        own_sems,
        x_send,
        x_recv,
        spill_sems,
    ) = rest[2 + len(NAMES) :]
    s = lax.axis_index("slab")
    c = lax.axis_index("col")

    in_copies = [
        pltpu.make_async_copy(source, target, in_sems.at[at])
        for at, (source, target) in enumerate(
            ((boxes_in, boxes), (counts_in, counts), (doses_in, doses_own))
        )
    ]
    for copy in in_copies:
        copy.start()
    const_copies = {}
    for at, name in enumerate(NAMES):
        source = constants_in[name]
        source = source.at[c] if name == "classes" else source
        const_copies[name] = pltpu.make_async_copy(source, held_in[name], const_sems.at[at])
        const_copies[name].start()

    def near(offset, col):
        return (lax.rem(s + offset + N_SLAB, N_SLAB), col)

    def remote(src, dst, send_sem, recv_sem, device):
        return pltpu.make_async_remote_copy(
            src_ref=src,
            dst_ref=dst,
            send_sem=send_sem,
            recv_sem=recv_sem,
            device_id=device,
            device_id_type=MESH,
        )

    here = 4 * s + c
    upper = s // 64

    def t_target(k):
        if k in (1, 2, 3):
            m, place, opposite, col = here % 256, upper, 0, k
        elif k in (5, 6, 7):
            m, place, opposite, col = (511 - here) % 256, 1 - upper, 1, 8 - k
        elif k == 4:
            m, place, opposite, col = here + upper * (511 - 2 * here), 1, upper, 0
        else:
            m, place, opposite, col = (here + upper * (512 - 2 * here)) % 256, 0, upper, 0
        return m // 2, col, 4 * (m % 2) + 2 * place + opposite

    def t_source(pp, place, opposite):
        p = 2 * s + pp
        if opposite:
            other = 511 - (p + 256 * place)
            zero_col = 511 - p if place else 512 - p - 256 * jnp.where(p == 0, 1, 0)
        else:
            other = p + 256 * place
            zero_col = p
        m = jnp.where(c == 0, zero_col, other)
        return m // 4, m % 4

    barrier = pltpu.get_barrier_semaphore()

    def greet(step, carry):
        pl.semaphore_signal(
            barrier,
            inc=1,
            device_id=(lax.rem(s + step, N_SLAB), c),
            device_id_type=MESH,
        )
        return carry

    lax.fori_loop(32, N_SLAB, greet, 0)
    lax.fori_loop(1, 32, greet, 0)
    for offset in range(-2, 3):
        for step in range(1, N_COL):
            pl.semaphore_signal(
                barrier,
                inc=1,
                device_id=near(offset, lax.rem(c + step, N_COL)),
                device_id_type=MESH,
            )
    for pp in range(2):
        for place in range(2):
            for opposite in range(2):
                from_slab, from_col = t_source(pp, place, opposite)
                away = 4 * from_slab + from_col != here

                @pl.when(away)
                def _(device=(from_slab, from_col)):
                    pl.semaphore_signal(barrier, inc=1, device_id=device, device_id_type=MESH)

    for copy in in_copies:
        copy.wait()
    box_own = boxes[...].astype(F32)
    slot_id = lax.broadcasted_iota(jnp.int32, (1, SLOTS), 1)
    dose = jnp.where(slot_id < counts[...], doses_own[...], 0.0)
    pack[0:4, :] = box_own
    pack[4:8, :] = jnp.broadcast_to(dose, (4, SLOTS))
    shots[8 + c] = pack[...]

    expected = 15 + N_SLAB - 1
    for k in range(8):
        to_slab, to_col, _ = t_target(k)
        expected = expected + jnp.where(4 * to_slab + to_col != here, 1, 0)
    pl.semaphore_wait(barrier, expected)

    shot_copies = []
    for d in range(4):
        for step in range(N_COL):
            if d != 2 or step:
                shot_copies.append(
                    remote(
                        pack,
                        shots.at[4 * d + c],
                        shot_send.at[4 * d + step],
                        shot_recv.at[4 * d + c],
                        near(2 - d, lax.rem(c + step, N_COL)),
                    )
                )
    for copy in shot_copies:
        copy.start()

    t_copies = []
    for k in range(8):
        to_slab, to_col, slot = t_target(k)
        away = 4 * to_slab + to_col != here
        row = transfer_ref.at[pl.ds(k, 1)]
        distant = remote(row, t_rows.at[slot], t_send.at[k], t_recv.at[slot], (to_slab, to_col))
        local = pltpu.make_async_copy(row, t_rows.at[slot], t_recv.at[slot])
        t_copies.append((away, distant))

        @pl.when(away)
        def _(copy=distant):
            copy.start()

        @pl.when(jnp.logical_not(away))
        def _(copy=local):
            copy.start()

    def await_shots(ds):
        for d in ds:
            for step in range(N_COL):
                if d != 2 or step:
                    slot = 4 * d + lax.rem(c + step, N_COL)
                    remote(
                        pack, shots.at[slot], shot_send.at[0], shot_recv.at[slot], (s, c)
                    ).wait_recv()

    await_shots((1, 2))

    def pool_cover(col, carry):
        for d in (1, 2):
            box = jnp.transpose(shots[4 * d + col])
            start = jnp.broadcast_to(box[:, 2:3], (SLOTS, 128))
            end = jnp.broadcast_to(box[:, 3:4], (SLOTS, 128))

            def one(block, inner):
                lane = lax.broadcasted_iota(jnp.int32, (SLOTS, 128), 1) + block * 128
                left = (2 * lane + col * COLS).astype(F32)
                part = jnp.minimum(end, left + 2.0) - jnp.maximum(start, left)
                at = pl.multiple_of(block * 128, 128)
                cover_pool[col, (d - 1) * SLOTS : d * SLOTS, pl.ds(at, 128)] = jnp.maximum(
                    part, 0.0
                ).astype(BF16)
                return inner

            lax.fori_loop(0, 8, one, 0)
        return carry

    lax.fori_loop(0, N_COL, pool_cover, 0)

    def full_covers():
        await_shots((0, 3))
        for d in range(4):
            box = jnp.transpose(shots[4 * d + c])
            start = jnp.broadcast_to(box[:, 2:3], (SLOTS, 128))
            end = jnp.broadcast_to(box[:, 3:4], (SLOTS, 128))
            rows = slice(d * SLOTS, (d + 1) * SLOTS)

            def one(block, inner):
                lane = lax.broadcasted_iota(jnp.int32, (SLOTS, 128), 1) + block * 128
                pos = (lane + c * COLS).astype(F32)
                inside = (pos >= start) & (pos < end)
                at = pl.multiple_of(block * 128, 128)
                cover[rows, pl.ds(at, 128)] = jnp.where(inside, 1.0, 0.0).astype(BF16)
                return inner

            lax.fori_loop(0, COLS // 128, one, 0)
            for side in range(2):
                other = lax.rem(c + (1 if side else 3), N_COL)
                box = jnp.transpose(shots[4 * d + other])
                lane = lax.broadcasted_iota(jnp.int32, (SLOTS, 128), 1)
                pos = (lane + c * COLS + (COLS if side else -128)).astype(F32)
                inside = (pos >= box[:, 2:3]) & (pos < box[:, 3:4])
                cover_side[side, rows, :] = jnp.where(inside, 1.0, 0.0).astype(BF16)

    def blocks(row):
        return jnp.concatenate([row[:, b * 128 : (b + 1) * 128] for b in range(32)], axis=0)

    def make_filter():
        for slot in range(8):
            remote(
                transfer_ref.at[pl.ds(0, 1)],
                t_rows.at[slot],
                t_send.at[0],
                t_recv.at[slot],
                (s, c),
            ).wait_recv()
        unit = 1.0 / (LONG * LONG)
        lane = lax.broadcasted_iota(jnp.int32, (128, 128), 1)
        shared = jnp.where((lane < 64) & (here == 0), 1.0, 0.0)
        for pp in range(2):
            tables_of = []
            for opposite in range(2):
                first = blocks(t_rows[4 * pp + opposite])
                second = blocks(t_rows[4 * pp + 2 + opposite])
                stack = jnp.concatenate([first, first, second, second], axis=0)
                tables_of.append(jnp.transpose(stack) * unit)
            plus, minus = tables_of
            cross = jnp.zeros((128, 128), F32)
            if pp == 0:
                mean = 0.25 * (plus + minus)
                cross = 0.25 * (plus - minus) * shared
                plus = jnp.where(shared > 0.0, mean, plus)
                minus = jnp.where(shared > 0.0, mean, minus)
            filt[0, pl.ds(pp, 128, stride=2), :] = plus
            filt[1, pl.ds(pp, 128, stride=2), :] = minus
            mix[pl.ds(pp, 128, stride=2), :] = cross

    live = dose > 0.0
    area = (box_own[1:2] - box_own[0:1]) * (box_own[3:4] - box_own[2:3])

    def exchange(source, target, iteration, which):
        lane = which * ITERS + iteration

        def go(step, carry):
            there = lax.rem(s + step, N_SLAB)
            remote(
                source.at[iteration, pl.ds(2 * there, 2)],
                target.at[iteration, pl.ds(2 * s, 2)],
                slab_send.at[lane],
                slab_recv.at[lane],
                (there, c),
            ).start()
            return carry

        lax.fori_loop(32, N_SLAB, go, 0)
        lax.fori_loop(1, 32, go, 0)
        own = pltpu.make_async_copy(
            source.at[iteration, pl.ds(2 * s, 2)],
            target.at[iteration, pl.ds(2 * s, 2)],
            own_sems.at[lane],
        )
        own.start()
        whole = remote(
            source.at[iteration, pl.ds(0, 2 * N_SLAB - 2)],
            target.at[iteration, pl.ds(0, 2 * N_SLAB - 2)],
            slab_send.at[lane],
            slab_recv.at[lane],
            (lax.rem(s + 1, N_SLAB), c),
        )
        return own, whole

    def arrived(pair):
        own, whole = pair
        own.wait()
        whole.wait_recv()

    lane_id = lax.broadcasted_iota(jnp.int32, (256, 128), 1)
    sign = jnp.where(lane_id % 64 < 32, 1.0, -1.0)
    sent = []
    ready = set()

    def const(name):
        if name not in ready:
            ready.add(name)
            const_copies[name].wait()
        return held_in[name]

    for iteration in range(ITERS):

        def dose_of(slot):
            value = shots[slot, 4:5, :] if iteration == 0 else doses[slot]
            return value.astype(BF16).astype(F32)

        for col in range(N_COL):
            parts = []
            for d in (1, 2):
                slot = 4 * d + col
                top = 2 * lax.broadcasted_iota(jnp.int32, (32, SLOTS), 0) + s * ROWS
                top = top.astype(F32)
                part = jnp.minimum(shots[slot, 1:2, :], top + 2.0) - jnp.maximum(
                    shots[slot, 0:1, :], top
                )
                parts.append(jnp.maximum(part, 0.0) * (dose_of(slot) * 0.25))
            row_part = jnp.concatenate(parts, axis=1).astype(BF16)
            coarse[:, col * 1024 : (col + 1) * 1024] = mm(row_part, cover_pool[col])

        classes = const("classes")
        for place in range(2):
            real = jnp.zeros((32, 512), F32)
            imag = jnp.zeros((32, 512), F32)
            for q in range(8):
                block = slice(q * 512, (q + 1) * 512)
                x = coarse[:, block]
                real = real + x * classes[2 * place : 2 * place + 1, block]
                imag = imag - x * classes[2 * place + 1 : 2 * place + 2, block]
            at = place * 64
            real_high, real_low = split(real)
            imag_high, imag_low = split(imag)
            for base, re, im in ((at, real_high, imag_high), (128 + at, real_low, imag_low)):
                uv[base : base + 32, 0:512] = re
                uv[base + 32 : base + 64, 0:512] = im
                uv[base : base + 32, 512:1024] = im
                uv[base + 32 : base + 64, 512:1024] = -re
        column = const("column")
        both = mm(column[0], uv[...], ((1,), (1,)))
        spectrum = both[:, :128] + both[:, 128:] + mm(column[1], uv[0:128, :], ((1,), (1,)))
        alternate = const("alternate")
        both = mm(alternate[...], uv[:, 512:1024], ((1,), (1,)))
        nyquist = both[:, :128] + both[:, 128:]
        lane16 = lax.broadcasted_iota(jnp.int32, (16, 128), 1)
        chosen = (lane16 >= 32) & (lane16 < 64) & (c == 0)
        nyquist = jnp.where(chosen, nyquist, 0.0)
        scales = const("scales")
        scale = scales[0:1, :]
        send1[iteration] = (spectrum * scale).astype(BF16)
        send1[iteration, 0:16, :] = ((spectrum[0:16] - nyquist) * scale).astype(BF16)
        moving = exchange(send1, recv1, iteration, 0)
        sent.append(moving[1])

        if iteration == 0:
            full_covers()
        row_pos = (
            lax.broadcasted_iota(jnp.int32, (3 * ROWS, SLOTS), 0) + (s * ROWS - ROWS)
        ).astype(F32)
        for d in range(4):
            lanes = slice(d * SLOTS, (d + 1) * SLOTS)
            for place, step in enumerate((0, 3, 1)):
                slot = 4 * d + lax.rem(c + step, N_COL)
                inside = (row_pos >= shots[slot, 0:1, :]) & (row_pos < shots[slot, 1:2, :])
                value = jnp.where(inside, dose_of(slot), 0.0).astype(BF16)
                if place:
                    weights_side[place - 1, :, lanes] = value
                else:
                    weights[:, lanes] = value
        rows_band = const("rows_band")
        cols_band = const("cols_band")
        for side in range(2):
            at = side * (COLS + 128)
            block = mm(weights_side[side], cover_side[side]).astype(BF16)
            across[:, at : at + 128] = mm(rows_band[...], block).astype(BF16)

        def raster(block, carry):
            at = pl.multiple_of(block * 256, 256)
            tile = mm(weights[...], cover[:, pl.ds(at, 256)]).astype(BF16)
            across[:, pl.ds(at + 128, 256)] = mm(rows_band[...], tile).astype(BF16)
            return carry

        lax.fori_loop(0, COLS // 256, raster, 0)

        def blur(block, carry):
            at = pl.multiple_of(block * 128, 128)
            short[:, pl.ds(at, 128)] = mm(across[:, pl.ds(at, 384)], cols_band[...])
            return carry

        lax.fori_loop(0, COLS // 128, blur, 0)
        if iteration == 0:
            make_filter()
        slab = const("slab")
        small = const("small")
        twists = const("twists")

        arrived(moving)
        lines = recv1[iteration]
        both = mm(slab[0], lines) + mm(slab[1], lines)
        part = sign * both[:256]
        other = swap_parts(both[256:])
        turned = []
        for value in (sign * (part + other), part - other):
            turned.append(value * twists[0] + swap_parts(value) * twists[1])
        high, low = split(jnp.concatenate(turned, axis=0))
        value = mm(high, small[0]) + mm(low, small[0]) + mm(high, small[1])
        line, mirror = value[:256], value[256:]
        cross = mix[...]
        value = jnp.concatenate(
            [line * filt[0] + mirror * cross, mirror * filt[1] + line * cross], axis=0
        )
        high, low = split(value)
        value = mm(high, small[2]) + mm(low, small[2]) + mm(high, small[3])
        turned = []
        for part in (value[:256], value[256:]):
            turned.append(part * twists[2] - swap_parts(part) * twists[3])
        line, mirror = turned[0], sign * turned[1]
        high, low = split(line + mirror)
        both = mm(slab[0, 0:256], jnp.concatenate([high, low], axis=1))
        real_part = both[:, :128] + both[:, 128:] + mm(slab[1, 0:256], high)
        high, low = split(line - mirror)
        both = mm(slab[0, 256:512], jnp.concatenate([high, low], axis=1))
        imag_part = both[:, :128] + both[:, 128:] + mm(slab[1, 256:512], high)
        send2[iteration] = (real_part - sign * swap_parts(imag_part)).astype(BF16)
        moving = exchange(send2, recv2, iteration, 1)
        sent.append(moving[1])
        row_twice = const("row_twice")
        col_twice = const("col_twice")
        arrived(moving)

        held = recv2[iteration]
        both = mm(held, column[0], ((0,), (0,))) + mm(held, column[1], ((0,), (0,)))
        nyquist = mm(held[0:16], alternate[...], ((0,), (0,)))[32:64]
        points = []
        for place in range(2):
            re = slice(place * 64, place * 64 + 32)
            im = slice(place * 64 + 32, place * 64 + 64)
            points.append(
                (both[re, :512] - both[im, 512:], both[re, 512:] + both[im, :512])
            )
        points[0] = (points[0][0] + jnp.where(c == 0, nyquist, 0.0), points[0][1])

        x_copies = []
        for step in (2, 1, 3, 0):
            quarter = lax.rem(c + step, N_COL)
            for half in range(2):
                at = pl.multiple_of(quarter * 1024 + half * 512, 512)
                total = jnp.zeros((32, 512), F32)
                for place in range(2):
                    total = total + (
                        points[place][0] * classes[2 * place : 2 * place + 1, pl.ds(at, 512)]
                        - points[place][1]
                        * classes[2 * place + 1 : 2 * place + 2, pl.ds(at, 512)]
                    )
                field_out[iteration, step, :, half * 512 : (half + 1) * 512] = total.astype(BF16)
            if step:
                copy = remote(
                    field_out.at[iteration, step],
                    field.at[iteration, step],
                    x_send.at[iteration, step],
                    x_recv.at[iteration, step],
                    (s, quarter),
                )
                copy.start()
                x_copies.append(copy)
        back = field_out[iteration, 0].astype(F32)
        for step, copy in zip((2, 1, 3), x_copies):
            copy.wait_recv()
            back = back + field[iteration, step].astype(F32)
        row = lax.broadcasted_iota(jnp.int32, (32, 1024), 0).astype(F32)
        back = back * jnp.exp(row * (-math.log(2.0) / 32.0))

        high, low = split(back)
        high = mm(row_twice[...], high).astype(BF16)
        low = mm(row_twice[...], low).astype(BF16)
        for block in range(8):
            lanes = slice(block * 128, (block + 1) * 128)
            wide = slice(block * 256, (block + 1) * 256)
            value = (
                short[:, wide] + mm(high[:, lanes], col_twice[...]) + mm(low[:, lanes], col_twice[...])
            )
            if iteration == ITERS - 1:
                exposure_ref[:, wide] = value
            exposure_bf[:, wide] = value.astype(BF16)

        measured = mm(exposure_bf[...], cover[SLOTS : 3 * SLOTS, :], ((1,), (1,)))
        row_pos = (lax.broadcasted_iota(jnp.int32, (ROWS, SLOTS), 0) + s * ROWS).astype(F32)
        for d in (1, 2):
            slot = 4 * d + c
            inside = (row_pos >= shots[slot, 0:1, :]) & (row_pos < shots[slot, 1:2, :])
            part = jnp.where(inside, measured[:, (d - 1) * SLOTS : d * SLOTS], 0.0)
            sums_out[iteration, d - 1 : d, :] = jnp.sum(part, axis=0, keepdims=True)
        sent.extend(x_copies)
        if iteration == 0:
            for offset in (2, -2, 1, -1, 0):
                for step in range(N_COL):
                    if offset or step:
                        copy = remote(
                            sums_out.at[iteration],
                            sums.at[4 * (2 - offset) + c],
                            sums_send.at[4 * (2 - offset) + step],
                            sums_recv.at[4 * (2 - offset) + c],
                            near(offset, lax.rem(c + step, N_COL)),
                        )
                        copy.start()
                        sent.append(copy)
            sums[8 + c] = sums_out[iteration]
            for place in range(5):
                for step in range(N_COL):
                    if place != 2 or step:
                        slot = 4 * place + lax.rem(c + step, N_COL)
                        remote(
                            sums_out.at[iteration],
                            sums.at[slot],
                            sums_send.at[0],
                            sums_recv.at[slot],
                            (s, c),
                        ).wait_recv()
            for slot in range(4 * N_COL):
                box = shots[slot]
                whole_area = (box[1:2] - box[0:1]) * (box[3:4] - box[2:3])
                average = (sums[slot, 1:2, :] + sums[slot + N_COL, 0:1, :]) / whole_area
                past = box[4:5]
                doses[slot] = jnp.where(
                    past > 0.0, past * jnp.exp(RELAX * (TARGET_LEVEL - average)), 0.0
                )
        else:
            copy = remote(
                sums_out.at[iteration],
                spill,
                spill_sems.at[0],
                spill_sems.at[1],
                near(-1, c),
            )
            copy.start()
            for other in sent:
                other.wait_send()
            for other in shot_copies:
                other.wait_send()
            for away, other in t_copies:

                @pl.when(away)
                def _(other=other):
                    other.wait_send()

            copy.wait()
            average = (sums_out[iteration, 1:2, :] + spill[0:1, :]) / area
            dose = doses[8 + c]
            dosage_ref[...] = jnp.where(
                live, dose * jnp.exp(RELAX * (TARGET_LEVEL - average)), 0.0
            )


def per_device(shot_boxes, shot_counts, shot_doses, transfer):
    t = tables()
    constants = [jnp.asarray(t[name]) for name in NAMES]
    vmem = pl.BlockSpec(memory_space=pltpu.VMEM)
    stay = pl.BlockSpec(memory_space=pl.ANY)
    dma = pltpu.SemaphoreType.DMA
    held = [
        pltpu.VMEM(value.shape[1:] if name == "classes" else value.shape, value.dtype)
        for name, value in zip(NAMES, constants)
    ]
    dosage, exposure = pl.pallas_call(
        kernel,
        out_shape=(
            jax.ShapeDtypeStruct((1, SLOTS), F32),
            jax.ShapeDtypeStruct((ROWS, COLS), F32),
        ),
        in_specs=[stay] * (4 + len(constants)),
        out_specs=(vmem, vmem),
        scratch_shapes=[
            *held,
            pltpu.VMEM((4, SLOTS), jnp.int32),
            pltpu.VMEM((1, 1), jnp.int32),
            pltpu.VMEM((1, SLOTS), F32),
            pltpu.VMEM((8, SLOTS), F32),
            pltpu.VMEM((16, 8, SLOTS), F32),
            pltpu.VMEM((16, 1, SLOTS), F32),
            pltpu.VMEM((ITERS, 2, SLOTS), F32),
            pltpu.VMEM((20, 2, SLOTS), F32),
            pltpu.VMEM((2, SLOTS), F32),
            pltpu.VMEM((8, 1, LONG), F32),
            pltpu.VMEM((2, 256, 128), F32),
            pltpu.VMEM((256, 128), F32),
            pltpu.VMEM((4 * SLOTS, COLS), BF16),
            pltpu.VMEM((2, 4 * SLOTS, 128), BF16),
            pltpu.VMEM((N_COL, 2 * SLOTS, 1024), BF16),
            pltpu.VMEM((3 * ROWS, 4 * SLOTS), BF16),
            pltpu.VMEM((2, 3 * ROWS, 4 * SLOTS), BF16),
            pltpu.VMEM((ROWS, COLS + 256), BF16),
            pltpu.VMEM((ROWS, COLS), F32),
            pltpu.VMEM((ROWS, COLS), BF16),
            pltpu.VMEM((32, LONG), F32),
            pltpu.VMEM((256, 1024), BF16),
            pltpu.VMEM((ITERS, 2 * N_SLAB, 128), BF16),
            pltpu.VMEM((ITERS, 2 * N_SLAB, 128), BF16),
            pltpu.VMEM((ITERS, 2 * N_SLAB, 128), BF16),
            pltpu.VMEM((ITERS, 2 * N_SLAB, 128), BF16),
            pltpu.VMEM((ITERS, N_COL, 32, 1024), BF16),
            pltpu.VMEM((ITERS, N_COL, 32, 1024), BF16),
            dma((len(NAMES),)),
            dma((3,)),
            dma((16,)),
            dma((16,)),
            dma((20,)),
            dma((20,)),
            dma((8,)),
            dma((8,)),
            dma((2 * ITERS,)),
            dma((2 * ITERS,)),
            dma((2 * ITERS,)),
            dma((ITERS, N_COL)),
            dma((ITERS, N_COL)),
            dma((2,)),
        ],
        compiler_params=pltpu.CompilerParams(
            collective_id=0, has_side_effects=True, vmem_limit_bytes=60 << 20
        ),
        name="dose_correction",
    )(shot_boxes, shot_counts, shot_doses.reshape(1, SLOTS), transfer, *constants)
    return dosage.reshape(SLOTS), exposure


def solution(mesh):
    placed = (
        P(None, ("slab", "col")),
        P("slab", "col"),
        P(("slab", "col")),
        P(("slab", "col"), None),
    )
    return jax.shard_map(
        per_device,
        mesh=mesh,
        in_specs=placed,
        out_specs=(P(("slab", "col")), P("slab", "col")),
        check_vma=False,
    )
```

time: 124 us -> 101 us (0.81)
  Pallas kernels: 108 us -> 96.5 us
  local copies, waits for them, and re-layouts: 12.8 us -> 3.1 us
  other arithmetic: 1.38 us -> 0 us
    pallas_call x1, Pallas kernels: 108 us -> 96.5 us  [per_device(): pl.pallas_call(kernel, out_shape=(jax.ShapeDtypeStruct((1, SLOTS), F32),...]
    unnamed x25 -> x4, local copies, waits for them, and re-layouts: 12.8 us -> 3.1 us
where the time goes in v1:
time: 101 us
  Pallas kernels  96.5 us (96%)
  local copies, waits for them, and re-layouts  3.1 us (3%)
  between operations  1.29 us (1%)
    pallas_call x1, Pallas kernels, per_device(): pl.pallas_call(kernel, out_shape=(jax.ShapeDtypeStruct((1, SLOTS), F32),...  96.5 us
    unnamed x4, local copies, waits for them, and re-layouts  3.1 us

profile of v1, /device:TPU:1, one launch (start us, length us, event | category | flops | bytes accessed | tf_op | source)
XLA Modules:
  0.0 100.9 jit_solution(110707379911136175)
XLA Ops:
  1.3 96.5 %dose_correction.1 = (f32[1,256]{1,0:T(1,128)}, f32[64,2048]{1,0:T(8,128)}) custom-call(s32[4,256]{1,0:T(4,128)} %boxes_in.1, s32[1,1]{1,0:T(1,128)S(6)} %copy.19.counts_in, f32[1,256]{1,0:T(1,128)} %bitcast.2, f32[8,4096]{1,0:T(8,128)} %transfer_ref.1, bf16[2,256,1024]{2,1,0:T(8,128)(2,1)} %constant.22.clone.rest_0_, ...), custom_call_target="tpu_custom_call" | custom-call | tf_op jit(solution)/shard_map/dose_correction/pallas_call | solution.py:721
  97.8 0.0 copy-start
  97.8 0.7 copy-done
  98.5 0.6 copy.20
  99.1 1.9 %copy.21 = f32[64,2048]{1,0:T(8,128)} copy(f32[64,2048]{1,0:T(8,128)} %get-tuple-element.9) | data formatting | bytes 1048576
Async XLA Ops:
  97.8 0.7 copy-start

commit v2 on v1

--- a/solution.py
+++ b/solution.py
@@ -47,12 +47,13 @@
     slab = np.concatenate([np.kron(np.cos(slab_angle), pair), np.kron(np.sin(slab_angle), pair)])
     small = turn / 32 * ((np.arange(32)[:, None] * np.arange(32)[None, :]) % 32)
     cos, sin = np.cos(small), np.sin(small)
-    forward = np.kron(pair, np.block([[cos, -sin], [sin, cos]]))
-    backward = np.kron(pair, np.block([[cos, sin], [-sin, cos]]))
+    cos, sin = np.kron(pair, cos), np.kron(pair, sin)
+    forward = np.block([[cos, -sin], [sin, cos]])
+    backward = np.block([[cos, sin], [-sin, cos]])
     lane = np.arange(128)
     scale = 2.0 ** ((lane % 32) / 32.0)
     twist = turn / LONG * np.repeat(np.arange(128), 2)[:, None] * (lane % 32)[None, :]
-    sign = np.where(lane % 64 < 32, 1.0, -1.0)
+    sign = np.where(lane < 64, 1.0, -1.0)
     twists = np.stack(
         [
             np.cos(twist) / scale,
@@ -75,7 +76,9 @@
     for c in range(128):
         cols_band[c + 64 : c + 64 + 2 * HALO + 1, c] = taps
     row_twice = (np.arange(ROWS)[:, None] // 2 == np.arange(32)[None, :]).astype(jnp.bfloat16)
-    col_twice = (np.arange(128)[:, None] == np.arange(256)[None, :] // 2).astype(jnp.bfloat16)
+    col_twice = (np.arange(256)[:, None] % 128 == np.arange(256)[None, :] // 2).astype(
+        jnp.bfloat16
+    )
     alternate = np.zeros((16, 512), jnp.bfloat16)
     alternate[0] = 1 - 2 * (np.arange(512) % 2)
     scales = np.stack([scale, np.zeros(128)] * 4).astype(np.float32)
@@ -119,12 +122,19 @@
 
 
 def swap_parts(x):
-    lane = lax.broadcasted_iota(jnp.int32, x.shape, x.ndim - 1)
-    return jnp.where(
-        lane % 64 < 32,
-        pltpu.roll(x, 96, x.ndim - 1),
-        pltpu.roll(x, 32, x.ndim - 1),
-    )
+    return pltpu.roll(x, 64, 1)
+
+
+def over_slabs(act):
+    def turn(group, carry):
+        for place in range(8):
+            act(group * 8 + place)
+        return carry
+
+    lax.fori_loop(6, 16, turn, 0)
+    lax.fori_loop(1, 6, turn, 0)
+    for step in range(1, 8):
+        act(step)
 
 
 def kernel(
@@ -240,17 +250,15 @@
 
     barrier = pltpu.get_barrier_semaphore()
 
-    def greet(step, carry):
+    def greet(step):
         pl.semaphore_signal(
             barrier,
             inc=1,
             device_id=(lax.rem(s + step, N_SLAB), c),
             device_id_type=MESH,
         )
-        return carry
-
-    lax.fori_loop(32, N_SLAB, greet, 0)
-    lax.fori_loop(1, 32, greet, 0)
+
+    over_slabs(greet)
     for offset in range(-2, 3):
         for step in range(1, N_COL):
             pl.semaphore_signal(
@@ -277,6 +285,65 @@
     pack[0:4, :] = box_own
     pack[4:8, :] = jnp.broadcast_to(dose, (4, SLOTS))
     shots[8 + c] = pack[...]
+
+    def from_block(col):
+        begins, ends, firsts = [], [], []
+        for d in (1, 2):
+            box = shots[4 * d + col]
+            begin = box[2:3] - (col * COLS).astype(F32)
+            first = jnp.floor(begin * (1.0 / 256.0))
+            begins.append(begin - first * 256.0 - 64.0)
+            ends.append(box[3:4] - (col * COLS).astype(F32) - first * 256.0 - 64.0)
+            firsts.append(first)
+        return tuple(jnp.concatenate(parts, axis=1) for parts in (begins, ends, firsts))
+
+    def pool_cover(col, carry):
+        begin, end, _ = from_block(col)
+        row = lax.broadcasted_iota(jnp.int32, (16, 2 * SLOTS), 0)
+        both = jnp.where(row == 0, begin, jnp.where(row == 1, end, 0.0)).astype(BF16)
+        row = lax.broadcasted_iota(jnp.int32, (16, 256), 0)
+        lane = lax.broadcasted_iota(jnp.int32, (16, 256), 1)
+        pick = jnp.where(row == lane // 128, 1.0, 0.0).astype(BF16)
+        wide = mm(both, pick, ((0,), (0,)))
+        begin, end = wide[:, :128], wide[:, 128:]
+        for part in range(2):
+            lane = lax.broadcasted_iota(jnp.int32, (2 * SLOTS, 128), 1)
+            left = (2 * lane + (256 * part - 64)).astype(F32)
+            inside = jnp.minimum(end, left + 2.0) - jnp.maximum(begin, left)
+            cover_pool[col, :, part * 128 : (part + 1) * 128] = jnp.maximum(inside, 0.0).astype(
+                BF16
+            )
+        return carry
+
+    def full_covers(ds):
+        for d in ds:
+            box = jnp.transpose(shots[4 * d + c])
+            start = jnp.broadcast_to(box[:, 2:3], (SLOTS, 128))
+            end = jnp.broadcast_to(box[:, 3:4], (SLOTS, 128))
+            rows = slice(d * SLOTS, (d + 1) * SLOTS)
+
+            def one(block, inner):
+                lane = lax.broadcasted_iota(jnp.int32, (SLOTS, 128), 1) + block * 128
+                pos = (lane + c * COLS).astype(F32)
+                inside = (pos >= start) & (pos < end)
+                at = pl.multiple_of(block * 128, 128)
+                cover[rows, pl.ds(at, 128)] = jnp.where(inside, 1.0, 0.0).astype(BF16)
+                return inner
+
+            lax.fori_loop(0, COLS // 128, one, 0)
+
+    def side_covers():
+        for d in range(4):
+            rows = slice(d * SLOTS, (d + 1) * SLOTS)
+            for side in range(2):
+                other = lax.rem(c + (1 if side else 3), N_COL)
+                box = jnp.transpose(shots[4 * d + other])
+                lane = lax.broadcasted_iota(jnp.int32, (SLOTS, 128), 1)
+                pos = (lane + c * COLS + (COLS if side else -128)).astype(F32)
+                inside = (pos >= box[:, 2:3]) & (pos < box[:, 3:4])
+                cover_side[side, rows, :] = jnp.where(inside, 1.0, 0.0).astype(BF16)
+
+    full_covers((2,))
 
     expected = 15 + N_SLAB - 1
     for k in range(8):
@@ -328,51 +395,7 @@
 
     await_shots((1, 2))
 
-    def pool_cover(col, carry):
-        for d in (1, 2):
-            box = jnp.transpose(shots[4 * d + col])
-            start = jnp.broadcast_to(box[:, 2:3], (SLOTS, 128))
-            end = jnp.broadcast_to(box[:, 3:4], (SLOTS, 128))
-
-            def one(block, inner):
-                lane = lax.broadcasted_iota(jnp.int32, (SLOTS, 128), 1) + block * 128
-                left = (2 * lane + col * COLS).astype(F32)
-                part = jnp.minimum(end, left + 2.0) - jnp.maximum(start, left)
-                at = pl.multiple_of(block * 128, 128)
-                cover_pool[col, (d - 1) * SLOTS : d * SLOTS, pl.ds(at, 128)] = jnp.maximum(
-                    part, 0.0
-                ).astype(BF16)
-                return inner
-
-            lax.fori_loop(0, 8, one, 0)
-        return carry
-
     lax.fori_loop(0, N_COL, pool_cover, 0)
-
-    def full_covers():
-        await_shots((0, 3))
-        for d in range(4):
-            box = jnp.transpose(shots[4 * d + c])
-            start = jnp.broadcast_to(box[:, 2:3], (SLOTS, 128))
-            end = jnp.broadcast_to(box[:, 3:4], (SLOTS, 128))
-            rows = slice(d * SLOTS, (d + 1) * SLOTS)
-
-            def one(block, inner):
-                lane = lax.broadcasted_iota(jnp.int32, (SLOTS, 128), 1) + block * 128
-                pos = (lane + c * COLS).astype(F32)
-                inside = (pos >= start) & (pos < end)
-                at = pl.multiple_of(block * 128, 128)
-                cover[rows, pl.ds(at, 128)] = jnp.where(inside, 1.0, 0.0).astype(BF16)
-                return inner
-
-            lax.fori_loop(0, COLS // 128, one, 0)
-            for side in range(2):
-                other = lax.rem(c + (1 if side else 3), N_COL)
-                box = jnp.transpose(shots[4 * d + other])
-                lane = lax.broadcasted_iota(jnp.int32, (SLOTS, 128), 1)
-                pos = (lane + c * COLS + (COLS if side else -128)).astype(F32)
-                inside = (pos >= box[:, 2:3]) & (pos < box[:, 3:4])
-                cover_side[side, rows, :] = jnp.where(inside, 1.0, 0.0).astype(BF16)
 
     def blocks(row):
         return jnp.concatenate([row[:, b * 128 : (b + 1) * 128] for b in range(32)], axis=0)
@@ -388,13 +411,13 @@
             ).wait_recv()
         unit = 1.0 / (LONG * LONG)
         lane = lax.broadcasted_iota(jnp.int32, (128, 128), 1)
-        shared = jnp.where((lane < 64) & (here == 0), 1.0, 0.0)
+        shared = jnp.where((lane % 64 < 32) & (here == 0), 1.0, 0.0)
         for pp in range(2):
             tables_of = []
             for opposite in range(2):
                 first = blocks(t_rows[4 * pp + opposite])
                 second = blocks(t_rows[4 * pp + 2 + opposite])
-                stack = jnp.concatenate([first, first, second, second], axis=0)
+                stack = jnp.concatenate([first, second, first, second], axis=0)
                 tables_of.append(jnp.transpose(stack) * unit)
             plus, minus = tables_of
             cross = jnp.zeros((128, 128), F32)
@@ -413,28 +436,26 @@
     def exchange(source, target, iteration, which):
         lane = which * ITERS + iteration
 
-        def go(step, carry):
+        def go(step):
             there = lax.rem(s + step, N_SLAB)
             remote(
-                source.at[iteration, pl.ds(2 * there, 2)],
-                target.at[iteration, pl.ds(2 * s, 2)],
+                source.at[iteration, there],
+                target.at[iteration, s],
                 slab_send.at[lane],
                 slab_recv.at[lane],
                 (there, c),
             ).start()
-            return carry
-
-        lax.fori_loop(32, N_SLAB, go, 0)
-        lax.fori_loop(1, 32, go, 0)
+
+        over_slabs(go)
         own = pltpu.make_async_copy(
-            source.at[iteration, pl.ds(2 * s, 2)],
-            target.at[iteration, pl.ds(2 * s, 2)],
+            source.at[iteration, s],
+            target.at[iteration, s],
             own_sems.at[lane],
         )
         own.start()
         whole = remote(
-            source.at[iteration, pl.ds(0, 2 * N_SLAB - 2)],
-            target.at[iteration, pl.ds(0, 2 * N_SLAB - 2)],
+            source.at[iteration, pl.ds(0, N_SLAB - 1)],
+            target.at[iteration, pl.ds(0, N_SLAB - 1)],
             slab_send.at[lane],
             slab_recv.at[lane],
             (lax.rem(s + 1, N_SLAB), c),
@@ -447,7 +468,7 @@
         whole.wait_recv()
 
     lane_id = lax.broadcasted_iota(jnp.int32, (256, 128), 1)
-    sign = jnp.where(lane_id % 64 < 32, 1.0, -1.0)
+    sign = jnp.where(lane_id < 64, 1.0, -1.0)
     sent = []
     ready = set()
 
@@ -473,8 +494,22 @@
                     shots[slot, 0:1, :], top
                 )
                 parts.append(jnp.maximum(part, 0.0) * (dose_of(slot) * 0.25))
-            row_part = jnp.concatenate(parts, axis=1).astype(BF16)
-            coarse[:, col * 1024 : (col + 1) * 1024] = mm(row_part, cover_pool[col])
+            row_part = jnp.concatenate(parts, axis=1)
+            first = from_block(jnp.int32(col))[2]
+            placed = jnp.concatenate(
+                [
+                    (row_part * jnp.where(first == float(b), 1.0, 0.0)).astype(BF16)
+                    for b in range(8)
+                ],
+                axis=0,
+            )
+            tile = mm(placed, cover_pool[col])
+            for b in range(8):
+                at = col * 1024 + b * 128
+                block = tile[b * 32 : (b + 1) * 32, :128]
+                if b:
+                    block = block + tile[(b - 1) * 32 : b * 32, 128:]
+                coarse[:, at : at + 128] = block
 
         classes = const("classes")
         for place in range(2):
@@ -485,14 +520,14 @@
                 x = coarse[:, block]
                 real = real + x * classes[2 * place : 2 * place + 1, block]
                 imag = imag - x * classes[2 * place + 1 : 2 * place + 2, block]
-            at = place * 64
+            at = place * 32
             real_high, real_low = split(real)
             imag_high, imag_low = split(imag)
             for base, re, im in ((at, real_high, imag_high), (128 + at, real_low, imag_low)):
                 uv[base : base + 32, 0:512] = re
-                uv[base + 32 : base + 64, 0:512] = im
+                uv[base + 64 : base + 96, 0:512] = im
                 uv[base : base + 32, 512:1024] = im
-                uv[base + 32 : base + 64, 512:1024] = -re
+                uv[base + 64 : base + 96, 512:1024] = -re
         column = const("column")
         both = mm(column[0], uv[...], ((1,), (1,)))
         spectrum = both[:, :128] + both[:, 128:] + mm(column[1], uv[0:128, :], ((1,), (1,)))
@@ -500,59 +535,25 @@
         both = mm(alternate[...], uv[:, 512:1024], ((1,), (1,)))
         nyquist = both[:, :128] + both[:, 128:]
         lane16 = lax.broadcasted_iota(jnp.int32, (16, 128), 1)
-        chosen = (lane16 >= 32) & (lane16 < 64) & (c == 0)
+        chosen = (lane16 >= 64) & (lane16 < 96) & (c == 0)
         nyquist = jnp.where(chosen, nyquist, 0.0)
         scales = const("scales")
         scale = scales[0:1, :]
-        send1[iteration] = (spectrum * scale).astype(BF16)
-        send1[iteration, 0:16, :] = ((spectrum[0:16] - nyquist) * scale).astype(BF16)
+        spectrum = jnp.concatenate([spectrum[0:16] - nyquist, spectrum[16:]], axis=0)
+        send1[iteration] = (spectrum * scale).astype(BF16).reshape(N_SLAB, 2, 128)
         moving = exchange(send1, recv1, iteration, 0)
         sent.append(moving[1])
 
         if iteration == 0:
-            full_covers()
-        row_pos = (
-            lax.broadcasted_iota(jnp.int32, (3 * ROWS, SLOTS), 0) + (s * ROWS - ROWS)
-        ).astype(F32)
-        for d in range(4):
-            lanes = slice(d * SLOTS, (d + 1) * SLOTS)
-            for place, step in enumerate((0, 3, 1)):
-                slot = 4 * d + lax.rem(c + step, N_COL)
-                inside = (row_pos >= shots[slot, 0:1, :]) & (row_pos < shots[slot, 1:2, :])
-                value = jnp.where(inside, dose_of(slot), 0.0).astype(BF16)
-                if place:
-                    weights_side[place - 1, :, lanes] = value
-                else:
-                    weights[:, lanes] = value
-        rows_band = const("rows_band")
-        cols_band = const("cols_band")
-        for side in range(2):
-            at = side * (COLS + 128)
-            block = mm(weights_side[side], cover_side[side]).astype(BF16)
-            across[:, at : at + 128] = mm(rows_band[...], block).astype(BF16)
-
-        def raster(block, carry):
-            at = pl.multiple_of(block * 256, 256)
-            tile = mm(weights[...], cover[:, pl.ds(at, 256)]).astype(BF16)
-            across[:, pl.ds(at + 128, 256)] = mm(rows_band[...], tile).astype(BF16)
-            return carry
-
-        lax.fori_loop(0, COLS // 256, raster, 0)
-
-        def blur(block, carry):
-            at = pl.multiple_of(block * 128, 128)
-            short[:, pl.ds(at, 128)] = mm(across[:, pl.ds(at, 384)], cols_band[...])
-            return carry
-
-        lax.fori_loop(0, COLS // 128, blur, 0)
-        if iteration == 0:
+            await_shots((0, 3))
+            full_covers((0, 1, 3))
+            side_covers()
             make_filter()
         slab = const("slab")
         small = const("small")
         twists = const("twists")
-
         arrived(moving)
-        lines = recv1[iteration]
+        lines = recv1[iteration].reshape(2 * N_SLAB, 128)
         both = mm(slab[0], lines) + mm(slab[1], lines)
         part = sign * both[:256]
         other = swap_parts(both[256:])
@@ -578,20 +579,57 @@
         high, low = split(line - mirror)
         both = mm(slab[0, 256:512], jnp.concatenate([high, low], axis=1))
         imag_part = both[:, :128] + both[:, 128:] + mm(slab[1, 256:512], high)
-        send2[iteration] = (real_part - sign * swap_parts(imag_part)).astype(BF16)
+        send2[iteration] = (
+            (real_part - sign * swap_parts(imag_part)).astype(BF16).reshape(N_SLAB, 2, 128)
+        )
         moving = exchange(send2, recv2, iteration, 1)
         sent.append(moving[1])
+
+        row_pos = (
+            lax.broadcasted_iota(jnp.int32, (3 * ROWS, SLOTS), 0) + (s * ROWS - ROWS)
+        ).astype(F32)
+        for d in range(4):
+            lanes = slice(d * SLOTS, (d + 1) * SLOTS)
+            for place, step in enumerate((0, 3, 1)):
+                slot = 4 * d + lax.rem(c + step, N_COL)
+                inside = (row_pos >= shots[slot, 0:1, :]) & (row_pos < shots[slot, 1:2, :])
+                value = jnp.where(inside, dose_of(slot), 0.0).astype(BF16)
+                if place:
+                    weights_side[place - 1, :, lanes] = value
+                else:
+                    weights[:, lanes] = value
+        rows_band = const("rows_band")
+        cols_band = const("cols_band")
+        for side in range(2):
+            at = side * (COLS + 128)
+            block = mm(weights_side[side], cover_side[side]).astype(BF16)
+            across[:, at : at + 128] = mm(rows_band[...], block).astype(BF16)
+
+        def raster(block, carry):
+            at = pl.multiple_of(block * 256, 256)
+            tile = mm(weights[...], cover[:, pl.ds(at, 256)]).astype(BF16)
+            across[:, pl.ds(at + 128, 256)] = mm(rows_band[...], tile).astype(BF16)
+            return carry
+
+        lax.fori_loop(0, COLS // 256, raster, 0)
+
+        def blur(block, carry):
+            at = pl.multiple_of(block * 128, 128)
+            short[:, pl.ds(at, 128)] = mm(across[:, pl.ds(at, 384)], cols_band[...])
+            return carry
+
+        lax.fori_loop(0, COLS // 128, blur, 0)
         row_twice = const("row_twice")
         col_twice = const("col_twice")
         arrived(moving)
 
-        held = recv2[iteration]
+        held = recv2[iteration].reshape(2 * N_SLAB, 128)
         both = mm(held, column[0], ((0,), (0,))) + mm(held, column[1], ((0,), (0,)))
-        nyquist = mm(held[0:16], alternate[...], ((0,), (0,)))[32:64]
+        nyquist = mm(held[0:16], alternate[...], ((0,), (0,)))[64:96]
         points = []
         for place in range(2):
-            re = slice(place * 64, place * 64 + 32)
-            im = slice(place * 64 + 32, place * 64 + 64)
+            re = slice(place * 32, place * 32 + 32)
+            im = slice(place * 32 + 64, place * 32 + 96)
             points.append(
                 (both[re, :512] - both[im, 512:], both[re, 512:] + both[im, :512])
             )
@@ -630,12 +668,14 @@
         high, low = split(back)
         high = mm(row_twice[...], high).astype(BF16)
         low = mm(row_twice[...], low).astype(BF16)
+        pieces = [slice(block * 128, (block + 1) * 128) for block in range(8)]
+        stacked = jnp.concatenate(
+            [jnp.concatenate([high[:, p], low[:, p]], axis=1) for p in pieces], axis=0
+        )
+        twice = mm(stacked, col_twice[...])
         for block in range(8):
-            lanes = slice(block * 128, (block + 1) * 128)
             wide = slice(block * 256, (block + 1) * 256)
-            value = (
-                short[:, wide] + mm(high[:, lanes], col_twice[...]) + mm(low[:, lanes], col_twice[...])
-            )
+            value = short[:, wide] + twice[block * ROWS : (block + 1) * ROWS]
             if iteration == ITERS - 1:
                 exposure_ref[:, wide] = value
             exposure_bf[:, wide] = value.astype(BF16)
@@ -703,9 +743,8 @@
             copy.wait()
             average = (sums_out[iteration, 1:2, :] + spill[0:1, :]) / area
             dose = doses[8 + c]
-            dosage_ref[...] = jnp.where(
-                live, dose * jnp.exp(RELAX * (TARGET_LEVEL - average)), 0.0
-            )
+            dose = jnp.where(live, dose * jnp.exp(RELAX * (TARGET_LEVEL - average)), 0.0)
+            dosage_ref[...] = dose.reshape(SLOTS)
 
 
 def per_device(shot_boxes, shot_counts, shot_doses, transfer):
@@ -721,7 +760,7 @@
     dosage, exposure = pl.pallas_call(
         kernel,
         out_shape=(
-            jax.ShapeDtypeStruct((1, SLOTS), F32),
+            jax.ShapeDtypeStruct((SLOTS,), F32),
             jax.ShapeDtypeStruct((ROWS, COLS), F32),
         ),
         in_specs=[stay] * (4 + len(constants)),
@@ -742,7 +781,7 @@
             pltpu.VMEM((256, 128), F32),
             pltpu.VMEM((4 * SLOTS, COLS), BF16),
             pltpu.VMEM((2, 4 * SLOTS, 128), BF16),
-            pltpu.VMEM((N_COL, 2 * SLOTS, 1024), BF16),
+            pltpu.VMEM((N_COL, 2 * SLOTS, 256), BF16),
             pltpu.VMEM((3 * ROWS, 4 * SLOTS), BF16),
             pltpu.VMEM((2, 3 * ROWS, 4 * SLOTS), BF16),
             pltpu.VMEM((ROWS, COLS + 256), BF16),
@@ -750,10 +789,10 @@
             pltpu.VMEM((ROWS, COLS), BF16),
             pltpu.VMEM((32, LONG), F32),
             pltpu.VMEM((256, 1024), BF16),
-            pltpu.VMEM((ITERS, 2 * N_SLAB, 128), BF16),
-            pltpu.VMEM((ITERS, 2 * N_SLAB, 128), BF16),
-            pltpu.VMEM((ITERS, 2 * N_SLAB, 128), BF16),
-            pltpu.VMEM((ITERS, 2 * N_SLAB, 128), BF16),
+            pltpu.VMEM((ITERS, N_SLAB, 2, 128), BF16),
+            pltpu.VMEM((ITERS, N_SLAB, 2, 128), BF16),
+            pltpu.VMEM((ITERS, N_SLAB, 2, 128), BF16),
+            pltpu.VMEM((ITERS, N_SLAB, 2, 128), BF16),
             pltpu.VMEM((ITERS, N_COL, 32, 1024), BF16),
             pltpu.VMEM((ITERS, N_COL, 32, 1024), BF16),
             dma((len(NAMES),)),
@@ -776,7 +815,7 @@
         ),
         name="dose_correction",
     )(shot_boxes, shot_counts, shot_doses.reshape(1, SLOTS), transfer, *constants)
-    return dosage.reshape(SLOTS), exposure
+    return dosage, exposure
 
 
 def solution(mesh):

time: 101 us -> 88.6 us (0.88)
  Pallas kernels: 96.5 us -> 84 us
    pallas_call x1, Pallas kernels: 96.5 us -> 84 us  [per_device(): pl.pallas_call(kernel, out_shape=(jax.ShapeDtypeStruct((SLOTS,), F32), ja...]
where the time goes in v2:
time: 88.6 us; the launch traced here: 88.4 us
  Pallas kernels  84 us (95%)
  local copies, waits for them, and re-layouts  3.1 us (3%)
  between operations  1.29 us (1%)
    pallas_call x1, Pallas kernels, per_device(): pl.pallas_call(kernel, out_shape=(jax.ShapeDtypeStruct((SLOTS,), F32), ja...  84 us
    unnamed x4, local copies, waits for them, and re-layouts  3.1 us

profile of v2, /device:TPU:1, one launch (start us, length us, event | category | flops | bytes accessed | tf_op | source)
XLA Modules:
  0.0 88.4 jit_solution(11035536296460250405)
XLA Ops:
  1.3 84.0 %dose_correction.1 = (f32[256]{0:T(256)}, f32[64,2048]{1,0:T(8,128)}) custom-call(s32[4,256]{1,0:T(4,128)} %boxes_in.1, s32[1,1]{1,0:T(1,128)S(6)} %copy.19.counts_in, f32[1,256]{1,0:T(1,128)} %bitcast.1, f32[8,4096]{1,0:T(8,128)} %transfer_ref.1, bf16[2,256,1024]{2,1,0:T(8,128)(2,1)} %constant.22.clone.rest_0_, ...), custom_call_target="tpu_custom_call" | custom-call | tf_op jit(solution)/shard_map/dose_correction/pallas_call | solution.py:760
  85.3 0.0 copy-start
  85.3 0.7 copy-done
  86.0 0.6 copy.20
  86.5 1.9 %copy.21 = f32[64,2048]{1,0:T(8,128)} copy(f32[64,2048]{1,0:T(8,128)} %get-tuple-element.5) | data formatting | bytes 1048576
Async XLA Ops:
  85.3 0.7 copy-start

commit v3 on v2

--- a/solution.py
+++ b/solution.py
@@ -30,6 +30,10 @@
     return high, low
 
 
+def joined(high, low):
+    return np.block([[high, low], [high, np.zeros_like(low)]])
+
+
 def blur_taps():
     pos = np.arange(-HALO, HALO + 1).astype(np.float32)
     spread = np.float32(HALO / 3.0)
@@ -49,7 +53,7 @@
     cos, sin = np.cos(small), np.sin(small)
     cos, sin = np.kron(pair, cos), np.kron(pair, sin)
     forward = np.block([[cos, -sin], [sin, cos]])
-    backward = np.block([[cos, sin], [-sin, cos]])
+    backward = np.block([[cos, sin], [-sin, cos]]) * 4.0 ** ((np.arange(128) % 32) / 32.0)
     lane = np.arange(128)
     scale = 2.0 ** ((lane % 32) / 32.0)
     twist = turn / LONG * np.repeat(np.arange(128), 2)[:, None] * (lane % 32)[None, :]
@@ -58,8 +62,6 @@
         [
             np.cos(twist) / scale,
             np.sin(twist) * sign / scale,
-            np.cos(twist) * scale,
-            np.sin(twist) * sign * scale,
         ]
     ).astype(np.float32)
     classes = np.zeros((N_COL, 4, LONG), np.float32)
@@ -85,7 +87,7 @@
     return dict(
         column=np.stack(halves(column)),
         slab=np.stack(halves(slab)),
-        small=np.stack(halves(forward) + halves(backward)),
+        small=np.stack([joined(*halves(forward)), joined(*halves(backward))]),
         twists=twists,
         classes=classes,
         rows_band=rows_band,
@@ -123,6 +125,10 @@
 
 def swap_parts(x):
     return pltpu.roll(x, 64, 1)
+
+
+def around(place):
+    return jnp.where(place >= N_SLAB, place - N_SLAB, place)
 
 
 def over_slabs(act):
@@ -254,7 +260,7 @@
         pl.semaphore_signal(
             barrier,
             inc=1,
-            device_id=(lax.rem(s + step, N_SLAB), c),
+            device_id=(around(s + step), c),
             device_id_type=MESH,
         )
 
@@ -437,7 +443,7 @@
         lane = which * ITERS + iteration
 
         def go(step):
-            there = lax.rem(s + step, N_SLAB)
+            there = around(s + step)
             remote(
                 source.at[iteration, there],
                 target.at[iteration, s],
@@ -560,18 +566,18 @@
         turned = []
         for value in (sign * (part + other), part - other):
             turned.append(value * twists[0] + swap_parts(value) * twists[1])
-        high, low = split(jnp.concatenate(turned, axis=0))
-        value = mm(high, small[0]) + mm(low, small[0]) + mm(high, small[1])
+        value = mm(jnp.concatenate(split(jnp.concatenate(turned, axis=0)), axis=1), small[0])
+        value = value[:, :128] + value[:, 128:]
         line, mirror = value[:256], value[256:]
         cross = mix[...]
         value = jnp.concatenate(
             [line * filt[0] + mirror * cross, mirror * filt[1] + line * cross], axis=0
         )
-        high, low = split(value)
-        value = mm(high, small[2]) + mm(low, small[2]) + mm(high, small[3])
+        value = mm(jnp.concatenate(split(value), axis=1), small[1])
+        value = value[:, :128] + value[:, 128:]
         turned = []
         for part in (value[:256], value[256:]):
-            turned.append(part * twists[2] - swap_parts(part) * twists[3])
+            turned.append(part * twists[0] - swap_parts(part) * twists[1])
         line, mirror = turned[0], sign * turned[1]
         high, low = split(line + mirror)
         both = mm(slab[0, 0:256], jnp.concatenate([high, low], axis=1))

time: 88.6 us -> 87.9 us (level)
  no operation moved by 1% of the time
where the time goes in v3:
time: 87.9 us; the launch traced here: 87.8 us
  Pallas kernels  83.4 us (95%)
  local copies, waits for them, and re-layouts  3.1 us (4%)
  between operations  1.29 us (1%)
    pallas_call x1, Pallas kernels, per_device(): pl.pallas_call(kernel, out_shape=(jax.ShapeDtypeStruct((SLOTS,), F32), ja...  83.4 us
    unnamed x4, local copies, waits for them, and re-layouts  3.1 us

profile of v3, /device:TPU:1, one launch (start us, length us, event | category | flops | bytes accessed | tf_op | source)
XLA Modules:
  0.0 87.8 jit_solution(8046088602751293184)
XLA Ops:
  1.3 83.4 %dose_correction.1 = (f32[256]{0:T(256)}, f32[64,2048]{1,0:T(8,128)}) custom-call(s32[4,256]{1,0:T(4,128)} %boxes_in.1, s32[1,1]{1,0:T(1,128)S(6)} %copy.19.counts_in, f32[1,256]{1,0:T(1,128)} %bitcast.1, f32[8,4096]{1,0:T(8,128)} %transfer_ref.1, bf16[2,256,1024]{2,1,0:T(8,128)(2,1)} %constant.22.clone.rest_0_, ...), custom_call_target="tpu_custom_call" | custom-call | tf_op jit(solution)/shard_map/dose_correction/pallas_call | solution.py:766
  84.6 0.0 copy-start
  84.7 0.7 copy-done
  85.3 0.6 copy.20
  85.9 1.9 %copy.21 = f32[64,2048]{1,0:T(8,128)} copy(f32[64,2048]{1,0:T(8,128)} %get-tuple-element.5) | data formatting | bytes 1048576
Async XLA Ops:
  84.6 0.7 copy-start
